TPU v7x, 128 devices: a whole 4x4x4 slice. The times are simulated.
128 devices in a mesh: dp: 8 (over z, core), node: 16 (over x, y).
Axes of the slice: x: 4, y: 4, z: 4, core: 2. Of those that a mesh axis runs over, the one named last changes fastest.
Arguments:
- vertex_embeddings: bfloat16 [8, 8192, 768], P('dp', 'node'), may hold values from -12 to 12
- incoming_adjoint: bfloat16 [8, 8192, 768], P('dp', 'node'), may hold values from -6 to 6
- asking_projector_matrix: bfloat16 [768, 768], replicated, may hold values from -0.21875 to 0.21875
- lookup_projector_matrix: bfloat16 [768, 768], replicated, may hold values from -0.21875 to 0.21875
- content_projector_matrix: bfloat16 [768, 768], replicated, may hold values from -0.21875 to 0.21875
- final_projector_matrix: bfloat16 [768, 768], replicated, may hold values from -0.21875 to 0.21875
- grouped_vertex_permutation: int32 [8, 8192], P('dp'), may hold values from 0 to 8191, as said below
- listed_tiles: int32 [8, 32, 64, 4], P('dp'), may hold values from 0 to 63, as said below
- active_tile_tally: int32 [8, 32, 64], P('dp'), may hold values from 1 to 4, as said below
Outputs:
- sublayer_yield: bfloat16 [8, 8192, 768], P('dp', 'node')
- embedding_derivative: bfloat16 [8, 8192, 768], P('dp', 'node')
- grad_query: float32 [768, 768], replicated
- grad_key: float32 [768, 768], replicated
- grad_value: float32 [768, 768], replicated
- grad_out: float32 [768, 768], replicated
Inputs may be any that keep to these rules, and one draw needn't show every extreme that they name: `grouped_vertex_permutation`: each subgraph's row is a permutation of the 8192 nodes. listed_tiles[g, h, b, :] are 4 distinct key block numbers, the first of them b. `active_tile_tally`: for every subgraph and head some query block has 4.
All inputs are finite; a program needn't handle non-finite values.
Results may differ from a plain program's by a relative error of at most 0.015.
The roundings to bfloat16 on the way count: a program that leaves them out, or rounds other values in their place, can miss the bound.
Values may be sent and summed in bfloat16 or wider, within the bound.
No kernel may reach another device: no remote copies, remote signals or barrier semaphores. Data moves between devices by JAX's collectives and lax.ppermute only.
A program may use at most 128 MiB of HBM per device.

v0:
```python
import functools
import math

import jax
import jax.numpy as jnp
from jax import lax
from jax.experimental import pallas as pl
from jax.experimental.pallas import tpu as pltpu
from jax.sharding import PartitionSpec as P


H = 32
HD = 24
BLOCK = 128
ROW_UNROLL = 64
GROUP = (4, 4, 4, 3)
LOG2E = math.log2(math.e)
F32 = jnp.float32
BF16 = jnp.bfloat16
NT = (((1,), (1,)), ((), ()))
NN = (((1,), (0,)), ((), ()))


def dot(a, b, dims):
    return lax.dot_general(a, b, dims, preferred_element_type=F32)


def eye():
    r = lax.broadcasted_iota(jnp.int32, (BLOCK, BLOCK), 0)
    c = lax.broadcasted_iota(jnp.int32, (BLOCK, BLOCK), 1)
    return jnp.where(r == c, 1.0, 0.0).astype(BF16)


def attend_kernel(
    nblocks,
    slots,
    per_source,
    order_ref,
    ids_ref,
    count_ref,
    in_ref,
    out_ref,
    rows_a,
    rows_b,
    x_rows,
    rhs_score,
    kv_cols,
    oq_cols,
    acc,
    bucket,
    fill,
):
    scale = 1.0 / math.sqrt(HD)
    pad = jnp.zeros((BLOCK - 4 * HD, BLOCK), F32)
    pad_half = jnp.zeros((BLOCK - 4 * HD, BLOCK), BF16)
    gap = jnp.zeros((HD, BLOCK), F32)
    ident = eye()

    def to_rows(j, _):
        src = j // per_source
        col = pl.multiple_of((j % per_source) * BLOCK, BLOCK)
        at = pl.multiple_of(j * BLOCK, BLOCK)
        tall = jnp.concatenate([in_ref[src, :, pl.ds(col, BLOCK)], pad_half], axis=0)
        rows_a[pl.ds(at, BLOCK), :] = tall.astype(F32).T
        return 0

    lax.fori_loop(0, nblocks, to_rows, 0, unroll=8)

    def fetch(i, _):
        base = pl.multiple_of(i * ROW_UNROLL, ROW_UNROLL)
        where = order_ref.at[pl.ds(base, ROW_UNROLL)]
        for u in range(ROW_UNROLL):
            rows_b[pl.ds(base + u, 1), :] = rows_a[pl.ds(where[u], 1), :]
        return 0

    lax.fori_loop(0, nblocks * BLOCK // ROW_UNROLL, fetch, 0)

    def forms(j, _):
        at = pl.multiple_of(j * BLOCK, BLOCK)
        rows = rows_b[pl.ds(at, BLOCK), :]
        x_rows[j] = rows.astype(BF16)
        tall = rows.T
        q_t, up_t = tall[0:HD], tall[3 * HD : 4 * HD]
        score = jnp.concatenate([gap, q_t, gap, gap, pad], axis=0).astype(BF16)
        value = jnp.concatenate([gap, gap, up_t, gap, pad], axis=0).astype(BF16)
        rhs_score[j] = jnp.concatenate([score, value], axis=1)
        kv_cols[j] = tall[HD : 3 * HD].astype(BF16)
        acc[j] = jnp.zeros((BLOCK, BLOCK), F32)
        return 0

    lax.fori_loop(0, nblocks, forms, 0, unroll=8)

    for c in range(slots):
        fill[c] = 0

    def place(i, _):
        c = count_ref[i] - 1
        n = fill[c]
        bucket[c * nblocks + n] = i
        fill[c] = n + 1
        return 0

    lax.fori_loop(0, nblocks, place, 0)

    lane = lax.broadcasted_iota(jnp.int32, (BLOCK, BLOCK), 1)
    q_lanes = lane < HD
    up_lanes = (lane >= 3 * HD) & (lane < 4 * HD)

    def attend(items, live):
        where = [(b, [ids_ref[b * slots + m] for m in range(live)]) for b in items]
        both = []
        for b, ids in where:
            keys = jnp.concatenate([x_rows[j] for j in ids], axis=0)
            both.append(dot(keys, rhs_score[b], NN))
        back = []
        for s in both:
            score = s[:, :BLOCK]
            dprob = s[:, BLOCK:]
            top = jnp.max(score, axis=0, keepdims=True)
            expo = jnp.exp2((score - top) * (scale * LOG2E))
            prob = expo * (1.0 / jnp.sum(expo, axis=0, keepdims=True))
            delta = jnp.sum(prob * dprob, axis=0, keepdims=True)
            dscore = prob * (dprob - delta) * scale
            back.append(jnp.concatenate([dscore.astype(BF16), prob.astype(BF16)], axis=1))
        for (b, ids), g in zip(where, back):
            cols = jnp.concatenate([kv_cols[j] for j in ids], axis=1)
            oq = dot(cols, g, NN)
            oq_cols[b] = jnp.concatenate([oq[:HD, :BLOCK], oq[HD:, BLOCK:]], axis=0).astype(BF16)
        grads = []
        for (b, ids), g in zip(where, back):
            rows = x_rows[b]
            zero = jnp.zeros_like(rows)
            weight = jnp.concatenate(
                [jnp.where(q_lanes, rows, zero), jnp.where(up_lanes, rows, zero)], axis=0
            )
            grads.append(dot(g, weight, NN))
        for (b, ids), d in zip(where, grads):
            for m, j in enumerate(ids):
                acc[j] += d[m * BLOCK : (m + 1) * BLOCK]

    for c in range(slots):
        base = c * nblocks
        total = fill[c]

        def group(t, _, c=c, base=base):
            attend([bucket[base + GROUP[c] * t + u] for u in range(GROUP[c])], c + 1)
            return 0

        lax.fori_loop(0, total // GROUP[c], group, 0)

        def single(t, _, c=c, base=base):
            attend([bucket[base + t]], c + 1)
            return 0

        lax.fori_loop(total // GROUP[c] * GROUP[c], total, single, 0)

    def results(j, _):
        at = pl.multiple_of(j * BLOCK, BLOCK)
        oq = oq_cols[j].astype(F32)
        tall = jnp.concatenate([gap, oq, gap, pad], axis=0).astype(BF16)
        rows_b[pl.ds(at, BLOCK), :] = tall.astype(F32).T + acc[j]
        return 0

    lax.fori_loop(0, nblocks, results, 0, unroll=8)

    def put(i, _):
        base = pl.multiple_of(i * ROW_UNROLL, ROW_UNROLL)
        where = order_ref.at[pl.ds(base, ROW_UNROLL)]
        for u in range(ROW_UNROLL):
            rows_a[pl.ds(where[u], 1), :] = rows_b[pl.ds(base + u, 1), :]
        return 0

    lax.fori_loop(0, nblocks * BLOCK // ROW_UNROLL, put, 0)

    def to_cols(j, _):
        dst = j // per_source
        col = pl.multiple_of((j % per_source) * BLOCK, BLOCK)
        at = pl.multiple_of(j * BLOCK, BLOCK)
        tall = rows_a[pl.ds(at, BLOCK), :].T
        out_ref[dst, :, pl.ds(col, BLOCK)] = tall[: 4 * HD].astype(BF16)
        return 0

    lax.fori_loop(0, nblocks, to_cols, 0, unroll=8)


def attend_head(order, ids, counts, arrived):
    sources, feats, width = arrived.shape
    total = sources * width
    nblocks = total // BLOCK
    slots = ids.shape[-1]
    smem = pl.BlockSpec(memory_space=pltpu.SMEM)
    vmem = pl.BlockSpec(memory_space=pltpu.VMEM)
    return pl.pallas_call(
        functools.partial(attend_kernel, nblocks, slots, width // BLOCK),
        out_shape=jax.ShapeDtypeStruct((sources, feats, width), BF16),
        in_specs=[smem] * 3 + [vmem],
        out_specs=vmem,
        scratch_shapes=[
            pltpu.VMEM((total, BLOCK), F32),
            pltpu.VMEM((total, BLOCK), F32),
            pltpu.VMEM((nblocks, BLOCK, BLOCK), BF16),
            pltpu.VMEM((nblocks, BLOCK, 2 * BLOCK), BF16),
            pltpu.VMEM((nblocks, 2 * HD, BLOCK), BF16),
            pltpu.VMEM((nblocks, 2 * HD, BLOCK), BF16),
            pltpu.VMEM((nblocks, BLOCK, BLOCK), F32),
            pltpu.SMEM((slots * nblocks,), jnp.int32),
            pltpu.SMEM((slots,), jnp.int32),
        ],
        compiler_params=pltpu.CompilerParams(vmem_limit_bytes=40000 * 1024),
        cost_estimate=pl.CostEstimate(
            flops=30_000_000_000, bytes_accessed=100_000_000, transcendentals=0
        ),
        name="attend",
    )(order, ids.reshape(-1), counts, arrived)


def project(weight, rows):
    return lax.dot_general(
        weight, rows, (((0,), (1,)), ((), ())), preferred_element_type=jnp.float32
    ).astype(jnp.bfloat16)


def ring(axis_name, size, to_coord, to_index, flip):
    pairs = []
    for i in range(size):
        c = to_coord(i)
        pairs.append((i, to_index(i, 3 - c if flip else c ^ 1)))
    return axis_name, pairs


def torus(dp, node):
    side = 4
    z = lambda i: i // 2
    x = lambda i: i // side
    y = lambda i: i % side
    axes = {
        "z": ("dp", z, lambda i, c: c * 2 + i % 2),
        "x": ("node", x, lambda i, c: c * side + i % side),
        "y": ("node", y, lambda i, c: (i // side) * side + c),
    }
    sizes = {"dp": dp, "node": node}
    out = {}
    for key, (name, coord, index) in axes.items():
        pairings = [ring(name, sizes[name], coord, index, flip) for flip in (False, True)]
        out[key] = (coord(lax.axis_index(name)), pairings)
    return out


def pick(arr, bit):
    two = arr.reshape(2, arr.shape[0] // 2, arr.shape[1])
    return jnp.where(bit == 0, two[0], two[1])


def join(mine, other, bit):
    low = jnp.where(bit == 0, mine, other)
    high = jnp.where(bit == 0, other, mine)
    return jnp.concatenate([low, high], axis=0)


def add(a, b):
    return (a.astype(F32) + b.astype(F32)).astype(BF16)


class Sum:
    def __init__(self):
        self.dp, node = lax.axis_size("dp"), lax.axis_size("node")
        axes = torus(self.dp, node)
        self.core = lax.axis_index("dp") % 2
        self.other_core = [(i, i ^ 1) for i in range(self.dp)]

        def plan(key):
            coord, pairings = axes[key]
            low = ((coord == 1) | (coord == 2)).astype(jnp.int32)
            return list(zip((low, (coord >= 2).astype(jnp.int32)), pairings))

        wide = [plan("z"), plan("x")]
        self.wide = [p[::-1] if m else p for p in wide for m in range(2)]
        self.mid = plan("y")

    def swap(self, arr, step):
        return lax.ppermute(arr, step[1][0], step[1][1])

    def halve(self, arr, step):
        return pick(arr, step[0]), self.swap(pick(arr, 1 - step[0]), step)

    def start(self, head, grads, also=None):
        low, high = [jnp.concatenate(grads[i : i + 2]) for i in (0, 2)]
        send = jnp.where(self.core == 0, high, low)
        keep = jnp.where(self.core == 0, low, high)
        total = add(keep, lax.ppermute(send, "dp", self.other_core))
        deep = total.shape[0] // 2
        chunks = [total[:deep], total[deep:]]
        wide = self.wide[2 * head : 2 * head + 2]
        for n in range(2):
            pairs = [self.halve(c, w[n]) for c, w in zip(chunks, wide)]
            if n == 0 and also is not None:
                pairs[1], also = lax.optimization_barrier((pairs[1], also))
            chunks = [add(*p) for p in pairs]
        return chunks, also

    def end(self, chunks):
        cols = chunks[0].shape[1]
        quarter = chunks[0].shape[0] // 4
        both = jnp.stack([c.reshape(4, quarter, cols) for c in chunks], axis=1)
        both = both.reshape(16 * quarter, cols)
        for step in self.mid:
            both = add(*self.halve(both, step))
        part = [both[: 2 * quarter], both[2 * quarter :]]
        for n in range(2):
            part = [add(part[i], self.swap(part[i], self.wide[2 - 2 * i][n])) for i in range(2)]
        both = jnp.concatenate(part)
        for step in reversed(self.mid):
            both = join(both, self.swap(both, step), step[0])
        both = both.reshape(4, 4, quarter, cols)
        chunks = [both[:, k].reshape(4 * quarter, cols) for k in range(4)]
        for n in (1, 0):
            chunks = [join(c, self.swap(c, w[n]), w[n][0]) for c, w in zip(chunks, self.wide)]
        part = [jnp.concatenate([chunks[i], chunks[2 + i]]) for i in range(2)]
        return part, [lax.ppermute(p, "dp", self.other_core) for p in part]


def finish_kernel(factor, core_ref, q_mine, k_mine, v_mine, o_mine, q_oth, k_oth, v_oth, o_oth, *outs):
    core = core_ref[0]

    def write(q, k, v, o):
        for src, out in zip((q, k, v), outs):
            out[...] = src[...].T.astype(F32) * factor
        outs[3][...] = o[...].astype(F32) * factor

    @pl.when(core == 0)
    def _():
        write(q_mine, k_mine, v_oth, o_oth)

    @pl.when(core != 0)
    def _():
        write(q_oth, k_oth, v_mine, o_mine)


def finish(core, part, other, factor):
    size = part[0].shape[0]
    wide = pl.BlockSpec((BLOCK, size), lambda i, c: (i, 0))

    def taken(first, tall):
        def at(i, c):
            row = jnp.where(c[0] == first, i, 0)
            return (0, row) if tall else (row, 0)

        return pl.BlockSpec((size, BLOCK) if tall else (BLOCK, size), at)

    specs = [taken(f, t) for f, t in ((0, 1), (0, 1), (1, 1), (1, 0))]
    specs += [taken(f, t) for f, t in ((1, 1), (1, 1), (0, 1), (0, 0))]
    args = [part[0], part[1], part[0], part[1], other[0], other[1], other[0], other[1]]
    return pl.pallas_call(
        functools.partial(finish_kernel, factor),
        out_shape=[jax.ShapeDtypeStruct((size, size), F32)] * 4,
        grid_spec=pltpu.PrefetchScalarGridSpec(
            num_scalar_prefetch=1,
            grid=(size // BLOCK,),
            in_specs=specs,
            out_specs=[wide] * 4,
        ),
        name="finish",
    )(core.reshape(1), *args)


def local(
    vertex_embeddings,
    incoming_adjoint,
    asking_projector_matrix,
    lookup_projector_matrix,
    content_projector_matrix,
    final_projector_matrix,
    grouped_vertex_permutation,
    listed_tiles,
    active_tile_tally,
):
    rows = vertex_embeddings[0]
    cotan = incoming_adjoint[0]
    parts = lax.axis_size("node")
    halves = H // parts
    cut = parts * HD
    width = rows.shape[0]
    total = parts * width

    def swap(arr):
        return lax.all_to_all(arr, "node", split_axis=0, concat_axis=0, tiled=True)

    me = lax.axis_index("node")
    order = grouped_vertex_permutation[0]
    dims_first = (((0,), (0,)), ((), ()))
    dims_back = (((0,), (1,)), ((), ()))
    arrived = []
    for n in range(halves):
        own = slice(n * cut, (n + 1) * cut)
        sent = [
            project(asking_projector_matrix[:, own], rows),
            project(lookup_projector_matrix[:, own], rows),
            project(content_projector_matrix[:, own], rows),
            dot(final_projector_matrix[own], cotan, NT).astype(BF16),
        ]
        part = jnp.stack([t.reshape(parts, HD, width) for t in sent], axis=1)
        arrived.append(swap(part.reshape(parts, 4 * HD, width)))
    done = []
    for n in range(halves):
        head = n * parts + me
        ids = lax.dynamic_index_in_dim(listed_tiles[0], head, 0, keepdims=False)
        live = lax.dynamic_index_in_dim(active_tile_tally[0], head, 0, keepdims=False)
        done.append(attend_head(order, ids, live, arrived[n]))
    first, done[1] = lax.optimization_barrier((swap(done[0]), done[1]))
    second = swap(done[1])

    def split(arr):
        arr = arr.reshape(parts, 4, HD, width)
        return [arr[:, i].reshape(cut, width) for i in range(4)]

    def grads_of(dk, dq, out, dv):
        pairs = ((dq, rows), (dk, rows), (dv, rows), (out, cotan))
        return [dot(a, b, NN).astype(BF16) for a, b in pairs]

    reduce = Sum()
    nodes = [split(first)]
    chunks, _ = reduce.start(0, grads_of(*nodes[0]))
    second, chunks = lax.optimization_barrier((second, chunks))
    nodes.append(split(second))
    dk, dq, out, dv = [jnp.concatenate(t, axis=0) for t in zip(*nodes)]
    result = lax.dot_general(
        out, final_projector_matrix, dims_first, preferred_element_type=jnp.float32
    ).astype(jnp.bfloat16)
    backward = (
        lax.dot_general(dq, asking_projector_matrix, dims_back, preferred_element_type=jnp.float32)
        + lax.dot_general(dk, lookup_projector_matrix, dims_back, preferred_element_type=jnp.float32)
        + lax.dot_general(dv, content_projector_matrix, dims_back, preferred_element_type=jnp.float32)
    ).astype(jnp.bfloat16)
    late, (result, backward) = reduce.start(1, grads_of(*nodes[1]), (result, backward))
    part, other = reduce.end(chunks + late)
    factor = 1.0 / math.sqrt(lax.axis_size("dp") * total)
    weights = finish(reduce.core, part, other, factor)
    return (result[None], backward[None], *weights)


def solution(mesh):
    placed = (
        P("dp", "node", None),
        P("dp", "node", None),
        P(),
        P(),
        P(),
        P(),
        P("dp", None),
        P("dp", None, None, None),
        P("dp", None, None),
    )
    return jax.shard_map(
        local,
        mesh=mesh,
        in_specs=placed,
        out_specs=(P("dp", "node", None), P("dp", "node", None), P(), P(), P(), P()),
        check_vma=False,
    )
```

profile of v0, /device:TPU:1, one launch (start us, length us, event | category | flops | bytes accessed | tf_op | source)
XLA Modules:
  0.0 280.7 jit_solution(3169988230733025158)
XLA Ops:
  8.0 7.6 %all-to-all-start = ((bf16[16,96,512]{2,1,0:T(8,128)(2,1)}), bf16[16,96,512]{2,1,0:T(8,128)(2,1)S(1)}, u32[]{:S(2)}, u32[]{:S(2)}) async-start(bf16[16,96,512]{2,1,0:T(8,128)(2,1)} %bitcast.125), calls=%async_computation | async-start | bytes 3145728 | tf_op jit(solution)/shard_map/all_to_all | solution.py:386
  23.5 12.8 %all-to-all-done.in_ref = bf16[16,96,512]{2,1,0:T(8,128)(2,1)S(1)} async-done(((bf16[16,96,512]{2,1,0:T(8,128)(2,1)}), bf16[16,96,512]{2,1,0:T(8,128)(2,1)S(1)}, u32[]{:S(2)}, u32[]{:S(2)}) %all-to-all-start) | async-done | bytes 1572896 | tf_op jit(solution)/shard_map/all_to_all | solution.py:386
  36.3 5.5 %all-to-all-start.2 = ((bf16[16,96,512]{2,1,0:T(8,128)(2,1)}), bf16[16,96,512]{2,1,0:T(8,128)(2,1)}, u32[]{:S(2)}, u32[]{:S(2)}) async-start(bf16[16,96,512]{2,1,0:T(8,128)(2,1)} %bitcast.128), calls=%async_computation.2 | async-start | bytes 3145728 | tf_op jit(solution)/shard_map/all_to_all | solution.py:386
  41.8 38.8 %attend.2 = bf16[16,96,512]{2,1,0:T(8,128)(2,1)S(1)} custom-call(s32[8192]{0:T(1024)S(1)} %bitcast.123, s32[256]{0:T(256)S(1)} %reshape.110.ids_ref, s32[64]{0:T(128)S(1)} %get-tuple-element.80.count_ref, bf16[16,96,512]{2,1,0:T(8,128)(2,1)S(1)} %all-to-all-done.in_ref), custom_call_target="tpu_custom_call" | custom-call | flops 30000001024 | bytes 100000000 | tf_op jit(solution)/shard_map/attend/pallas_call | solution.py:193
  81.7 6.7 %all-to-all-start.1 = ((bf16[16,96,512]{2,1,0:T(8,128)(2,1)}), bf16[16,96,512]{2,1,0:T(8,128)(2,1)S(1)}, u32[]{:S(2)}, u32[]{:S(2)}) async-start(bf16[16,96,512]{2,1,0:T(8,128)(2,1)} %copy-done.1), calls=%async_computation.1 | async-start | bytes 3145728 | tf_op jit(solution)/shard_map/all_to_all | solution.py:386
  88.5 42.2 %attend.3 = bf16[16,96,512]{2,1,0:T(8,128)(2,1)} custom-call(s32[8192]{0:T(1024)S(1)} %bitcast.124, s32[256]{0:T(256)S(1)} %reshape.112.ids_ref, s32[64]{0:T(128)S(1)} %get-tuple-element.79.count_ref, bf16[16,96,512]{2,1,0:T(8,128)(2,1)} %all-to-all-done.2.in_ref), custom_call_target="tpu_custom_call" | custom-call | flops 30000001024 | bytes 100000000 | tf_op jit(solution)/shard_map/attend/pallas_call | solution.py:193
  133.7 3.8 %collective-permute-start = (bf16[768,768]{1,0:T(8,128)(2,1)S(1)}, bf16[768,768]{1,0:T(8,128)(2,1)}, u32[]{:S(2)}, u32[]{:S(2)}) collective-permute-start(bf16[768,768]{1,0:T(8,128)(2,1)S(1)} %broadcast_select_fusion.1), channel_id=1, source_target_pairs={{0,16},{16,0},{32,48},{48,32},{64,80},{80,64},{96,112},{112,96},{1... | collective-permute-start | bytes 3538952 | tf_op jit(solution)/shard_map/ppermute | solution.py:290
  137.5 2.6 collective-permute-done
  143.0 3.7 %collective-permute-start.3 = (bf16[192,768]{1,0:T(8,128)(2,1)}, bf16[192,768]{1,0:T(8,128)(2,1)}, u32[]{:S(2)}, u32[]{:S(2)}) collective-permute-start(bf16[192,768]{1,0:T(8,128)(2,1)} %get-tuple-element.45), channel_id=1, source_target_pairs={{0,96},{16,112},{32,64},{48,80},{64,32},{80,48},{96,0},{112,16},{1... | collective-permute-start | bytes 884744 | tf_op jit(solution)/shard_map/ppermute | solution.py:281
  146.7 6.8 %all-to-all-start.3 = ((bf16[16,96,512]{2,1,0:T(8,128)(2,1)}), bf16[16,96,512]{2,1,0:T(8,128)(2,1)S(1)}, u32[]{:S(2)}, u32[]{:S(2)}) async-start(bf16[16,96,512]{2,1,0:T(8,128)(2,1)} %attend.3), calls=%async_computation.3 | async-start | bytes 3145728 | tf_op jit(solution)/shard_map/all_to_all | solution.py:386
  157.9 3.9 %collective-permute-done.2 = bf16[96,768]{1,0:T(8,128)(2,1)S(1)} collective-permute-done((bf16[96,768]{1,0:T(8,128)(2,1)S(1)}, bf16[96,768]{1,0:T(8,128)(2,1)S(1)}, u32[]{:S(2)}, u32[]{:S(2)}) %collective-permute-start.2) | collective-permute-done | bytes 147488 | tf_op jit(solution)/shard_map/ppermute | solution.py:281
  163.2 11.0 %all-to-all-done.3 = bf16[16,96,512]{2,1,0:T(8,128)(2,1)S(1)} async-done(((bf16[16,96,512]{2,1,0:T(8,128)(2,1)}), bf16[16,96,512]{2,1,0:T(8,128)(2,1)S(1)}, u32[]{:S(2)}, u32[]{:S(2)}) %all-to-all-start.3) | async-done | bytes 1572896 | tf_op jit(solution)/shard_map/all_to_all | solution.py:386
  178.9 4.0 %collective-permute-start.5 = (bf16[768,768]{1,0:T(8,128)(2,1)}, bf16[768,768]{1,0:T(8,128)(2,1)}, u32[]{:S(2)}, u32[]{:S(2)}) collective-permute-start(bf16[768,768]{1,0:T(8,128)(2,1)} %broadcast_select_fusion), channel_id=1, source_target_pairs={{0,16},{16,0},{32,48},{48,32},{64,80},{80,64},{96,112},{112,96},{1... | collective-permute-start | bytes 3538952 | tf_op jit(solution)/shard_map/ppermute | solution.py:290
  193.4 3.3 %collective-permute-done.7 = bf16[192,768]{1,0:T(8,128)(2,1)S(1)} collective-permute-done((bf16[192,768]{1,0:T(8,128)(2,1)S(1)}, bf16[192,768]{1,0:T(8,128)(2,1)S(1)}, u32[]{:S(2)}, u32[]{:S(2)}) %collective-permute-start.7) | collective-permute-done | bytes 294944 | tf_op jit(solution)/shard_map/ppermute | solution.py:281
  197.5 5.0 %collective-permute-done.6 = bf16[192,768]{1,0:T(8,128)(2,1)S(1)} collective-permute-done((bf16[192,768]{1,0:T(8,128)(2,1)S(1)}, bf16[192,768]{1,0:T(8,128)(2,1)S(1)}, u32[]{:S(2)}, u32[]{:S(2)}) %collective-permute-start.6) | collective-permute-done | bytes 294944 | tf_op jit(solution)/shard_map/ppermute | solution.py:281
  202.7 2.9 %collective-permute-done.8 = bf16[96,768]{1,0:T(8,128)(2,1)S(1)} collective-permute-done((bf16[96,768]{1,0:T(8,128)(2,1)S(1)}, bf16[96,768]{1,0:T(8,128)(2,1)S(1)}, u32[]{:S(2)}, u32[]{:S(2)}) %collective-permute-start.8) | collective-permute-done | bytes 147488 | tf_op jit(solution)/shard_map/ppermute | solution.py:281
  207.3 5.8 %collective-permute-done.10 = bf16[192,768]{1,0:T(8,128)(2,1)S(1)} collective-permute-done((bf16[192,768]{1,0:T(8,128)(2,1)S(1)}, bf16[192,768]{1,0:T(8,128)(2,1)S(1)}, u32[]{:S(2)}, u32[]{:S(2)}) %collective-permute-start.10) | collective-permute-done | bytes 294944 | tf_op jit(solution)/shard_map/ppermute | solution.py:281
  213.3 5.2 %collective-permute-done.11 = bf16[96,768]{1,0:T(8,128)(2,1)S(1)} collective-permute-done((bf16[96,768]{1,0:T(8,128)(2,1)S(1)}, bf16[96,768]{1,0:T(8,128)(2,1)S(1)}, u32[]{:S(2)}, u32[]{:S(2)}) %collective-permute-start.11) | collective-permute-done | bytes 147488 | tf_op jit(solution)/shard_map/ppermute | solution.py:281
  223.6 3.7 %collective-permute-done.13 = bf16[48,768]{1,0:T(8,128)(2,1)S(1)} collective-permute-done((bf16[48,768]{1,0:T(8,128)(2,1)S(1)}, bf16[48,768]{1,0:T(8,128)(2,1)S(1)}, u32[]{:S(2)}, u32[]{:S(2)}) %collective-permute-start.13) | collective-permute-done | bytes 73760 | tf_op jit(solution)/shard_map/ppermute | solution.py:281
  227.6 5.5 %collective-permute-done.16 = bf16[96,768]{1,0:T(8,128)(2,1)S(1)} collective-permute-done((bf16[96,768]{1,0:T(8,128)(2,1)S(1)}, bf16[96,768]{1,0:T(8,128)(2,1)S(1)}, u32[]{:S(2)}, u32[]{:S(2)}) %collective-permute-start.16) | collective-permute-done | bytes 147488 | tf_op jit(solution)/shard_map/ppermute | solution.py:281
  233.3 5.9 %collective-permute-done.17 = bf16[192,768]{1,0:T(8,128)(2,1)S(1)} collective-permute-done((bf16[192,768]{1,0:T(8,128)(2,1)S(1)}, bf16[192,768]{1,0:T(8,128)(2,1)S(1)}, u32[]{:S(2)}, u32[]{:S(2)}) %collective-permute-start.17) | collective-permute-done | bytes 294944 | tf_op jit(solution)/shard_map/ppermute | solution.py:281
  250.4 4.5 %collective-permute-done.25 = bf16[192,768]{1,0:T(8,128)(2,1)S(1)} collective-permute-done((bf16[192,768]{1,0:T(8,128)(2,1)S(1)}, bf16[192,768]{1,0:T(8,128)(2,1)S(1)}, u32[]{:S(2)}, u32[]{:S(2)}) %collective-permute-start.25) | collective-permute-done | bytes 294944 | tf_op jit(solution)/shard_map/ppermute | solution.py:281
  256.2 11.1 %collective-permute-start.27 = (bf16[768,768]{1,0:T(8,128)(2,1)S(1)}, bf16[768,768]{1,0:T(8,128)(2,1)S(1)}, u32[]{:S(2)}, u32[]{:S(2)}) collective-permute-start(bf16[768,768]{1,0:T(8,128)(2,1)S(1)} %pad_maximum_fusion.7.k_mine.o_mine), channel_id=1, source_target_pairs={{0,16},{16,0},{32,48},{48,32},{64,80},{80,64},{96,112},{112,96},{1... | collective-permute-start | bytes 3538952 | tf_op jit(solution)/shard_map/ppermute | solution.py:319
  272.5 8.0 %finish.1 = (f32[768,768]{1,0:T(8,128)}, f32[768,768]{1,0:T(8,128)}, f32[768,768]{1,0:T(8,128)}, f32[768,768]{1,0:T(8,128)}) custom-call(s32[1]{0:T(128)} %bitcast.35.core_ref, bf16[768,768]{1,0:T(8,128)(2,1)} %copy-done.4, bf16[768,768]{1,0:T(8,128)(2,1)} %copy-done.3, bf16[768,768]{1,0:T(8,128)(2,1)} %copy-done.4, bf16[768,768]{1,0:T(8,128)(2,1)} %copy-done.3, ...), custom_call_target="tpu_custom_call" | custom-call | tf_op jit(solution)/shard_map/finish/pallas_call | solution.py:353
  (187 shorter events, 68.7 us)
Async XLA Ops:
  8.0 28.3 %all-to-all-start = ((bf16[16,96,512]{2,1,0:T(8,128)(2,1)}), bf16[16,96,512]{2,1,0:T(8,128)(2,1)S(1)}, u32[]{:S(2)}, u32[]{:S(2)}) async-start(bf16[16,96,512]{2,1,0:T(8,128)(2,1)} %bitcast.125), calls=%async_computation | async-start | bytes 3145728 | tf_op jit(solution)/shard_map/all_to_all | solution.py:386
  36.3 45.4 %all-to-all-start.2 = ((bf16[16,96,512]{2,1,0:T(8,128)(2,1)}), bf16[16,96,512]{2,1,0:T(8,128)(2,1)}, u32[]{:S(2)}, u32[]{:S(2)}) async-start(bf16[16,96,512]{2,1,0:T(8,128)(2,1)} %bitcast.128), calls=%async_computation.2 | async-start | bytes 3145728 | tf_op jit(solution)/shard_map/all_to_all | solution.py:386
  81.7 49.0 %all-to-all-start.1 = ((bf16[16,96,512]{2,1,0:T(8,128)(2,1)}), bf16[16,96,512]{2,1,0:T(8,128)(2,1)S(1)}, u32[]{:S(2)}, u32[]{:S(2)}) async-start(bf16[16,96,512]{2,1,0:T(8,128)(2,1)} %copy-done.1), calls=%async_computation.1 | async-start | bytes 3145728 | tf_op jit(solution)/shard_map/all_to_all | solution.py:386
  133.7 6.5 %collective-permute-start = (bf16[768,768]{1,0:T(8,128)(2,1)S(1)}, bf16[768,768]{1,0:T(8,128)(2,1)}, u32[]{:S(2)}, u32[]{:S(2)}) collective-permute-start(bf16[768,768]{1,0:T(8,128)(2,1)S(1)} %broadcast_select_fusion.1), channel_id=1, source_target_pairs={{0,16},{16,0},{32,48},{48,32},{64,80},{80,64},{96,112},{112,96},{1... | collective-permute-start | bytes 3538952 | tf_op jit(solution)/shard_map/ppermute | solution.py:290
  143.0 11.0 %collective-permute-start.3 = (bf16[192,768]{1,0:T(8,128)(2,1)}, bf16[192,768]{1,0:T(8,128)(2,1)}, u32[]{:S(2)}, u32[]{:S(2)}) collective-permute-start(bf16[192,768]{1,0:T(8,128)(2,1)} %get-tuple-element.45), channel_id=1, source_target_pairs={{0,96},{16,112},{32,64},{48,80},{64,32},{80,48},{96,0},{112,16},{1... | collective-permute-start | bytes 884744 | tf_op jit(solution)/shard_map/ppermute | solution.py:281
  146.7 8.2 %collective-permute-start.1 = (bf16[192,768]{1,0:T(8,128)(2,1)}, bf16[192,768]{1,0:T(8,128)(2,1)}, u32[]{:S(2)}, u32[]{:S(2)}) collective-permute-start(bf16[192,768]{1,0:T(8,128)(2,1)} %get-tuple-element.46), channel_id=1, source_target_pairs={{0,32},{16,48},{32,0},{48,16},{64,96},{80,112},{96,64},{112,80},{1... | collective-permute-start | bytes 884744 | tf_op jit(solution)/shard_map/ppermute | solution.py:281
  146.7 27.5 %all-to-all-start.3 = ((bf16[16,96,512]{2,1,0:T(8,128)(2,1)}), bf16[16,96,512]{2,1,0:T(8,128)(2,1)S(1)}, u32[]{:S(2)}, u32[]{:S(2)}) async-start(bf16[16,96,512]{2,1,0:T(8,128)(2,1)} %attend.3), calls=%async_computation.3 | async-start | bytes 3145728 | tf_op jit(solution)/shard_map/all_to_all | solution.py:386
  156.2 5.6 %collective-permute-start.2 = (bf16[96,768]{1,0:T(8,128)(2,1)S(1)}, bf16[96,768]{1,0:T(8,128)(2,1)S(1)}, u32[]{:S(2)}, u32[]{:S(2)}) collective-permute-start(bf16[96,768]{1,0:T(8,128)(2,1)S(1)} %broadcast_select_fusion.31), channel_id=1, source_target_pairs={{0,96},{16,112},{32,64},{48,80},{64,32},{80,48},{96,0},{112,16},{1... | collective-permute-start | bytes 442376 | tf_op jit(solution)/shard_map/ppermute | solution.py:281
  178.9 7.3 %collective-permute-start.5 = (bf16[768,768]{1,0:T(8,128)(2,1)}, bf16[768,768]{1,0:T(8,128)(2,1)}, u32[]{:S(2)}, u32[]{:S(2)}) collective-permute-start(bf16[768,768]{1,0:T(8,128)(2,1)} %broadcast_select_fusion), channel_id=1, source_target_pairs={{0,16},{16,0},{32,48},{48,32},{64,80},{80,64},{96,112},{112,96},{1... | collective-permute-start | bytes 3538952 | tf_op jit(solution)/shard_map/ppermute | solution.py:290
  188.0 8.6 %collective-permute-start.7 = (bf16[192,768]{1,0:T(8,128)(2,1)S(1)}, bf16[192,768]{1,0:T(8,128)(2,1)S(1)}, u32[]{:S(2)}, u32[]{:S(2)}) collective-permute-start(bf16[192,768]{1,0:T(8,128)(2,1)S(1)} %get-tuple-element.40), channel_id=1, source_target_pairs={{0,4},{1,5},{2,6},{3,7},{4,0},{5,1},{6,2},{7,3},{8,12},{9,13},{10,... | collective-permute-start | bytes 884744 | tf_op jit(solution)/shard_map/ppermute | solution.py:281
  192.7 9.8 %collective-permute-start.6 = (bf16[192,768]{1,0:T(8,128)(2,1)S(1)}, bf16[192,768]{1,0:T(8,128)(2,1)S(1)}, u32[]{:S(2)}, u32[]{:S(2)}) collective-permute-start(bf16[192,768]{1,0:T(8,128)(2,1)S(1)} %get-tuple-element.42), channel_id=1, source_target_pairs={{0,12},{1,13},{2,14},{3,15},{4,8},{5,9},{6,10},{7,11},{8,4},{9,5},... | collective-permute-start | bytes 884744 | tf_op jit(solution)/shard_map/ppermute | solution.py:281
  196.8 8.9 %collective-permute-start.8 = (bf16[96,768]{1,0:T(8,128)(2,1)S(1)}, bf16[96,768]{1,0:T(8,128)(2,1)S(1)}, u32[]{:S(2)}, u32[]{:S(2)}) collective-permute-start(bf16[96,768]{1,0:T(8,128)(2,1)S(1)} %broadcast_select_fusion.23), channel_id=1, source_target_pairs={{0,12},{1,13},{2,14},{3,15},{4,8},{5,9},{6,10},{7,11},{8,4},{9,5},... | collective-permute-start | bytes 442376 | tf_op jit(solution)/shard_map/ppermute | solution.py:281
  206.9 6.2 %collective-permute-start.10 = (bf16[192,768]{1,0:T(8,128)(2,1)S(1)}, bf16[192,768]{1,0:T(8,128)(2,1)S(1)}, u32[]{:S(2)}, u32[]{:S(2)}) collective-permute-start(bf16[192,768]{1,0:T(8,128)(2,1)S(1)} %bitcast.163), channel_id=1, source_target_pairs={{0,1},{1,0},{2,3},{3,2},{4,5},{5,4},{6,7},{7,6},{8,9},{9,8},{10,11... | collective-permute-start | bytes 884744 | tf_op jit(solution)/shard_map/ppermute | solution.py:281
  213.2 5.3 %collective-permute-start.11 = (bf16[96,768]{1,0:T(8,128)(2,1)S(1)}, bf16[96,768]{1,0:T(8,128)(2,1)S(1)}, u32[]{:S(2)}, u32[]{:S(2)}) collective-permute-start(bf16[96,768]{1,0:T(8,128)(2,1)S(1)} %broadcast_select_fusion.19), channel_id=1, source_target_pairs={{0,3},{1,2},{2,1},{3,0},{4,7},{5,6},{6,5},{7,4},{8,11},{9,10},{10,... | collective-permute-start | bytes 442376 | tf_op jit(solution)/shard_map/ppermute | solution.py:281
  227.5 5.6 %collective-permute-start.16 = (bf16[96,768]{1,0:T(8,128)(2,1)S(1)}, bf16[96,768]{1,0:T(8,128)(2,1)S(1)}, u32[]{:S(2)}, u32[]{:S(2)}) collective-permute-start(bf16[96,768]{1,0:T(8,128)(2,1)S(1)} %pad_maximum_fusion.15), channel_id=1, source_target_pairs={{0,3},{1,2},{2,1},{3,0},{4,7},{5,6},{6,5},{7,4},{8,11},{9,10},{10,... | collective-permute-start | bytes 442376 | tf_op jit(solution)/shard_map/ppermute | solution.py:281
  233.2 5.9 %collective-permute-start.17 = (bf16[192,768]{1,0:T(8,128)(2,1)S(1)}, bf16[192,768]{1,0:T(8,128)(2,1)S(1)}, u32[]{:S(2)}, u32[]{:S(2)}) collective-permute-start(bf16[192,768]{1,0:T(8,128)(2,1)S(1)} %pad_maximum_fusion.10), channel_id=1, source_target_pairs={{0,1},{1,0},{2,3},{3,2},{4,5},{5,4},{6,7},{7,6},{8,9},{9,8},{10,11... | collective-permute-start | bytes 884744 | tf_op jit(solution)/shard_map/ppermute | solution.py:281
  239.3 5.3 %collective-permute-start.18 = (bf16[96,768]{1,0:T(8,128)(2,1)S(1)}, bf16[96,768]{1,0:T(8,128)(2,1)S(1)}, u32[]{:S(2)}, u32[]{:S(2)}) collective-permute-start(bf16[96,768]{1,0:T(8,128)(2,1)S(1)} %bitcast.152), channel_id=1, source_target_pairs={{0,96},{16,112},{32,64},{48,80},{64,32},{80,48},{96,0},{112,16},{1... | collective-permute-start | bytes 442376 | tf_op jit(solution)/shard_map/ppermute | solution.py:281
  240.0 9.4 %collective-permute-start.20 = (bf16[96,768]{1,0:T(8,128)(2,1)S(1)}, bf16[96,768]{1,0:T(8,128)(2,1)S(1)}, u32[]{:S(2)}, u32[]{:S(2)}) collective-permute-start(bf16[96,768]{1,0:T(8,128)(2,1)S(1)} %bitcast.149), channel_id=1, source_target_pairs={{0,12},{1,13},{2,14},{3,15},{4,8},{5,9},{6,10},{7,11},{8,4},{9,5},... | collective-permute-start | bytes 442376 | tf_op jit(solution)/shard_map/ppermute | solution.py:281
  242.6 4.9 %collective-permute-start.22 = (bf16[96,768]{1,0:T(8,128)(2,1)S(1)}, bf16[96,768]{1,0:T(8,128)(2,1)S(1)}, u32[]{:S(2)}, u32[]{:S(2)}) collective-permute-start(bf16[96,768]{1,0:T(8,128)(2,1)S(1)} %bitcast.150), channel_id=1, source_target_pairs={{0,32},{16,48},{32,0},{48,16},{64,96},{80,112},{96,64},{112,80},{1... | collective-permute-start | bytes 442376 | tf_op jit(solution)/shard_map/ppermute | solution.py:281
  244.7 22.7 %collective-permute-start.19 = (bf16[192,768]{1,0:T(8,128)(2,1)S(1)}, bf16[192,768]{1,0:T(8,128)(2,1)S(1)}, u32[]{:S(2)}, u32[]{:S(2)}) collective-permute-start(bf16[192,768]{1,0:T(8,128)(2,1)S(1)} %pad_maximum_fusion.11), channel_id=1, source_target_pairs={{0,32},{16,48},{32,0},{48,16},{64,96},{80,112},{96,64},{112,80},{1... | collective-permute-start | bytes 884744 | tf_op jit(solution)/shard_map/ppermute | solution.py:281
  246.9 8.0 %collective-permute-start.25 = (bf16[192,768]{1,0:T(8,128)(2,1)S(1)}, bf16[192,768]{1,0:T(8,128)(2,1)S(1)}, u32[]{:S(2)}, u32[]{:S(2)}) collective-permute-start(bf16[192,768]{1,0:T(8,128)(2,1)S(1)} %pad_maximum_fusion.14), channel_id=1, source_target_pairs={{0,12},{1,13},{2,14},{3,15},{4,8},{5,9},{6,10},{7,11},{8,4},{9,5},... | collective-permute-start | bytes 884744 | tf_op jit(solution)/shard_map/ppermute | solution.py:281
  247.5 8.4 %collective-permute-start.23 = (bf16[192,768]{1,0:T(8,128)(2,1)S(1)}, bf16[192,768]{1,0:T(8,128)(2,1)S(1)}, u32[]{:S(2)}, u32[]{:S(2)}) collective-permute-start(bf16[192,768]{1,0:T(8,128)(2,1)S(1)} %pad_maximum_fusion.13), channel_id=1, source_target_pairs={{0,96},{16,112},{32,64},{48,80},{64,32},{80,48},{96,0},{112,16},{1... | collective-permute-start | bytes 884744 | tf_op jit(solution)/shard_map/ppermute | solution.py:281
  249.4 18.0 %collective-permute-start.21 = (bf16[192,768]{1,0:T(8,128)(2,1)S(1)}, bf16[192,768]{1,0:T(8,128)(2,1)S(1)}, u32[]{:S(2)}, u32[]{:S(2)}) collective-permute-start(bf16[192,768]{1,0:T(8,128)(2,1)S(1)} %pad_maximum_fusion.12), channel_id=1, source_target_pairs={{0,4},{1,5},{2,6},{3,7},{4,0},{5,1},{6,2},{7,3},{8,12},{9,13},{10,... | collective-permute-start | bytes 884744 | tf_op jit(solution)/shard_map/ppermute | solution.py:281
  256.2 13.6 %collective-permute-start.27 = (bf16[768,768]{1,0:T(8,128)(2,1)S(1)}, bf16[768,768]{1,0:T(8,128)(2,1)S(1)}, u32[]{:S(2)}, u32[]{:S(2)}) collective-permute-start(bf16[768,768]{1,0:T(8,128)(2,1)S(1)} %pad_maximum_fusion.7.k_mine.o_mine), channel_id=1, source_target_pairs={{0,16},{16,0},{32,48},{48,32},{64,80},{80,64},{96,112},{112,96},{1... | collective-permute-start | bytes 3538952 | tf_op jit(solution)/shard_map/ppermute | solution.py:319
  (42 other events, 114.1 us)
where the time goes:
time: 282 us; the launch traced here: 281 us
  Pallas kernels  89 us (32%)
  waiting for transfers between devices  85 us (30%)
  starting transfers between devices  63.2 us (22%)
  matrix products  16.7 us (6%)
  other arithmetic  13.4 us (5%)
  local copies, waits for them, and re-layouts  11.7 us (4%)
    pallas_call x2, Pallas kernels, attend_head(): pl.pallas_call(functools.partial(attend_kernel, nblocks, slots, width //...  81 us
    ppermute x24, waiting for transfers between devices, swap(): return lax.ppermute(arr, step[1][0], step[1][1])  55.6 us
    all_to_all x4, starting transfers between devices, swap(): return lax.all_to_all(arr, 'node', split_axis=0, concat_axis=0, tiled=True)  26.5 us
    all_to_all x4, waiting for transfers between devices, swap(): return lax.all_to_all(arr, 'node', split_axis=0, concat_axis=0, tiled=True)  23.8 us
    ppermute x24, starting transfers between devices, swap(): return lax.ppermute(arr, step[1][0], step[1][1])  16.9 us
    ppermute x2, starting transfers between devices, end(): return (part, [lax.ppermute(p, 'dp', self.other_core) for p in part])  12 us
    unnamed x68, local copies, waits for them, and re-layouts  9.52 us
    pallas_call x1, Pallas kernels, finish(): pl.pallas_call(functools.partial(finish_kernel, factor), out_shape=[jax.S...  8.03 us
  transfers between devices with their start and end apart: 32, of which 24 were waited for; matrix products, arithmetic and copies ran while one was open for 6% of the time, Pallas kernels for 29%

commit v1 on v0

--- a/solution.py
+++ b/solution.py
@@ -283,18 +283,19 @@
     def halve(self, arr, step):
         return pick(arr, step[0]), self.swap(pick(arr, 1 - step[0]), step)
 
-    def start(self, head, grads, also=None):
+    def meet(self, grads):
         low, high = [jnp.concatenate(grads[i : i + 2]) for i in (0, 2)]
         send = jnp.where(self.core == 0, high, low)
         keep = jnp.where(self.core == 0, low, high)
-        total = add(keep, lax.ppermute(send, "dp", self.other_core))
-        deep = total.shape[0] // 2
-        chunks = [total[:deep], total[deep:]]
-        wide = self.wide[2 * head : 2 * head + 2]
+        return add(keep, lax.ppermute(send, "dp", self.other_core))
+
+    def start(self, totals, also):
+        deep = totals[0].shape[0] // 2
+        chunks = [t[m * deep : (m + 1) * deep] for t in totals for m in range(2)]
         for n in range(2):
-            pairs = [self.halve(c, w[n]) for c, w in zip(chunks, wide)]
-            if n == 0 and also is not None:
-                pairs[1], also = lax.optimization_barrier((pairs[1], also))
+            pairs = [self.halve(c, w[n]) for c, w in zip(chunks, self.wide)]
+            if n == 0:
+                pairs[3], also = lax.optimization_barrier((pairs[3], also))
             chunks = [add(*p) for p in pairs]
         return chunks, also
 
@@ -419,8 +420,8 @@
 
     reduce = Sum()
     nodes = [split(first)]
-    chunks, _ = reduce.start(0, grads_of(*nodes[0]))
-    second, chunks = lax.optimization_barrier((second, chunks))
+    total0 = reduce.meet(grads_of(*nodes[0]))
+    second, total0 = lax.optimization_barrier((second, total0))
     nodes.append(split(second))
     dk, dq, out, dv = [jnp.concatenate(t, axis=0) for t in zip(*nodes)]
     result = lax.dot_general(
@@ -431,8 +432,9 @@
         + lax.dot_general(dk, lookup_projector_matrix, dims_back, preferred_element_type=jnp.float32)
         + lax.dot_general(dv, content_projector_matrix, dims_back, preferred_element_type=jnp.float32)
     ).astype(jnp.bfloat16)
-    late, (result, backward) = reduce.start(1, grads_of(*nodes[1]), (result, backward))
-    part, other = reduce.end(chunks + late)
+    totals = [total0, reduce.meet(grads_of(*nodes[1]))]
+    chunks, (result, backward) = reduce.start(totals, (result, backward))
+    part, other = reduce.end(chunks)
     factor = 1.0 / math.sqrt(lax.axis_size("dp") * total)
     weights = finish(reduce.core, part, other, factor)
     return (result[None], backward[None], *weights)

time: 282 us -> 273 us (0.968)
  waiting for transfers between devices: 85 us -> 74 us
  starting transfers between devices: 63.2 us -> 69.8 us
  other arithmetic: 13.4 us -> 8.29 us
    ppermute x24, waiting for transfers between devices: 55.6 us -> 47.7 us  [swap(): return lax.ppermute(arr, step[1][0], step[1][1])]
    ppermute x2, starting transfers between devices: 12 us -> 16.5 us  [end(): return (part, [lax.ppermute(p, 'dp', self.other_core) for p in part])]
    convert_element_type x14, other arithmetic: 6.92 us -> 3.68 us  [add(): return (a.astype(F32) + b.astype(F32)).astype(BF16)]
    all_to_all x4, waiting for transfers between devices: 23.8 us -> 20.7 us  [swap(): return lax.all_to_all(arr, 'node', split_axis=0, concat_axis=0, tiled=True)]
    unnamed x68 -> x60, local copies, waits for them, and re-layouts: 9.52 us -> 9.91 us
  transfers between devices with their start and end apart: 32 -> 32, of which waited for: 24 -> 23; matrix products, arithmetic and copies ran while one was open for 6% -> 6% of each run, Pallas kernels for 29% -> 30%
where the time goes in v1:
time: 273 us; the launch traced here: 272 us
  Pallas kernels  89 us (33%)
  waiting for transfers between devices  74 us (27%)
  starting transfers between devices  69.8 us (26%)
  matrix products  16.1 us (6%)
  local copies, waits for them, and re-layouts  13.1 us (5%)
  other arithmetic  8.29 us (3%)
    pallas_call x2, Pallas kernels, attend_head(): pl.pallas_call(functools.partial(attend_kernel, nblocks, slots, width //...  81 us
    ppermute x24, waiting for transfers between devices, swap(): return lax.ppermute(arr, step[1][0], step[1][1])  47.7 us
    all_to_all x4, starting transfers between devices, swap(): return lax.all_to_all(arr, 'node', split_axis=0, concat_axis=0, tiled=True)  26.7 us
    all_to_all x4, waiting for transfers between devices, swap(): return lax.all_to_all(arr, 'node', split_axis=0, concat_axis=0, tiled=True)  20.7 us
    ppermute x24, starting transfers between devices, swap(): return lax.ppermute(arr, step[1][0], step[1][1])  17.8 us
    ppermute x2, starting transfers between devices, end(): return (part, [lax.ppermute(p, 'dp', self.other_core) for p in part])  16.5 us
    unnamed x60, local copies, waits for them, and re-layouts  9.91 us
    ppermute x2, starting transfers between devices, meet(): return add(keep, lax.ppermute(send, 'dp', self.other_core))  8.8 us
  transfers between devices with their start and end apart: 32, of which 23 were waited for; matrix products, arithmetic and copies ran while one was open for 6% of the time, Pallas kernels for 30%

profile of v1, /device:TPU:1, one launch (start us, length us, event | category | flops | bytes accessed | tf_op | source)
XLA Modules:
  0.0 271.9 jit_solution(13586495571010346831)
XLA Ops:
  8.0 7.6 %all-to-all-start = ((bf16[16,96,512]{2,1,0:T(8,128)(2,1)}), bf16[16,96,512]{2,1,0:T(8,128)(2,1)S(1)}, u32[]{:S(2)}, u32[]{:S(2)}) async-start(bf16[16,96,512]{2,1,0:T(8,128)(2,1)} %bitcast.126), calls=%async_computation | async-start | bytes 3145728 | tf_op jit(solution)/shard_map/all_to_all | solution.py:387
  23.5 12.8 %all-to-all-done.in_ref = bf16[16,96,512]{2,1,0:T(8,128)(2,1)S(1)} async-done(((bf16[16,96,512]{2,1,0:T(8,128)(2,1)}), bf16[16,96,512]{2,1,0:T(8,128)(2,1)S(1)}, u32[]{:S(2)}, u32[]{:S(2)}) %all-to-all-start) | async-done | bytes 1572896 | tf_op jit(solution)/shard_map/all_to_all | solution.py:387
  36.3 5.5 %all-to-all-start.2 = ((bf16[16,96,512]{2,1,0:T(8,128)(2,1)}), bf16[16,96,512]{2,1,0:T(8,128)(2,1)}, u32[]{:S(2)}, u32[]{:S(2)}) async-start(bf16[16,96,512]{2,1,0:T(8,128)(2,1)} %bitcast.128), calls=%async_computation.2 | async-start | bytes 3145728 | tf_op jit(solution)/shard_map/all_to_all | solution.py:387
  41.8 38.8 %attend.2 = bf16[16,96,512]{2,1,0:T(8,128)(2,1)S(1)} custom-call(s32[8192]{0:T(1024)S(1)} %bitcast.123, s32[256]{0:T(256)S(1)} %reshape.110.ids_ref, s32[64]{0:T(128)S(1)} %get-tuple-element.78.count_ref, bf16[16,96,512]{2,1,0:T(8,128)(2,1)S(1)} %all-to-all-done.in_ref), custom_call_target="tpu_custom_call" | custom-call | flops 30000001024 | bytes 100000000 | tf_op jit(solution)/shard_map/attend/pallas_call | solution.py:193
  81.7 6.7 %all-to-all-start.1 = ((bf16[16,96,512]{2,1,0:T(8,128)(2,1)}), bf16[16,96,512]{2,1,0:T(8,128)(2,1)S(1)}, u32[]{:S(2)}, u32[]{:S(2)}) async-start(bf16[16,96,512]{2,1,0:T(8,128)(2,1)} %copy-done.1), calls=%async_computation.1 | async-start | bytes 3145728 | tf_op jit(solution)/shard_map/all_to_all | solution.py:387
  88.5 42.2 %attend.3 = bf16[16,96,512]{2,1,0:T(8,128)(2,1)} custom-call(s32[8192]{0:T(1024)S(1)} %bitcast.124, s32[256]{0:T(256)S(1)} %reshape.112.ids_ref, s32[64]{0:T(128)S(1)} %get-tuple-element.77.count_ref, bf16[16,96,512]{2,1,0:T(8,128)(2,1)} %all-to-all-done.2.in_ref), custom_call_target="tpu_custom_call" | custom-call | flops 30000001024 | bytes 100000000 | tf_op jit(solution)/shard_map/attend/pallas_call | solution.py:193
  131.8 6.9 %all-to-all-start.3 = ((bf16[16,96,512]{2,1,0:T(8,128)(2,1)}), bf16[16,96,512]{2,1,0:T(8,128)(2,1)S(1)}, u32[]{:S(2)}, u32[]{:S(2)}) async-start(bf16[16,96,512]{2,1,0:T(8,128)(2,1)} %attend.3), calls=%async_computation.3 | async-start | bytes 3145728 | tf_op jit(solution)/shard_map/all_to_all | solution.py:387
  143.3 2.7 collective-permute-start
  146.0 2.6 collective-permute-done
  151.0 7.9 %all-to-all-done.3 = bf16[16,96,512]{2,1,0:T(8,128)(2,1)S(1)} async-done(((bf16[16,96,512]{2,1,0:T(8,128)(2,1)}), bf16[16,96,512]{2,1,0:T(8,128)(2,1)S(1)}, u32[]{:S(2)}, u32[]{:S(2)}) %all-to-all-start.3) | async-done | bytes 1572896 | tf_op jit(solution)/shard_map/all_to_all | solution.py:387
  164.8 3.1 %collective-permute-start.3 = (bf16[192,768]{1,0:T(8,128)(2,1)S(1)}, bf16[192,768]{1,0:T(8,128)(2,1)S(1)}, u32[]{:S(2)}, u32[]{:S(2)}) collective-permute-start(bf16[192,768]{1,0:T(8,128)(2,1)S(1)} %get-tuple-element.40), channel_id=1, source_target_pairs={{0,32},{16,48},{32,0},{48,16},{64,96},{80,112},{96,64},{112,80},{1... | collective-permute-start | bytes 884744 | tf_op jit(solution)/shard_map/ppermute | solution.py:281
  168.2 6.1 %collective-permute-start.1 = (bf16[768,768]{1,0:T(8,128)(2,1)S(1)}, bf16[768,768]{1,0:T(8,128)(2,1)S(1)}, u32[]{:S(2)}, u32[]{:S(2)}) collective-permute-start(bf16[768,768]{1,0:T(8,128)(2,1)S(1)} %broadcast_select_fusion), channel_id=1, source_target_pairs={{0,16},{16,0},{32,48},{48,32},{64,80},{80,64},{96,112},{112,96},{1... | collective-permute-start | bytes 3538952 | tf_op jit(solution)/shard_map/ppermute | solution.py:290
  187.5 3.0 %collective-permute-done.2 = bf16[192,768]{1,0:T(8,128)(2,1)S(1)} collective-permute-done((bf16[192,768]{1,0:T(8,128)(2,1)S(1)}, bf16[192,768]{1,0:T(8,128)(2,1)S(1)}, u32[]{:S(2)}, u32[]{:S(2)}) %collective-permute-start.2) | collective-permute-done | bytes 294944 | tf_op jit(solution)/shard_map/ppermute | solution.py:281
  190.7 2.6 collective-permute-done.8
  195.6 5.2 %collective-permute-done.10 = bf16[192,768]{1,0:T(8,128)(2,1)S(1)} collective-permute-done((bf16[192,768]{1,0:T(8,128)(2,1)S(1)}, bf16[192,768]{1,0:T(8,128)(2,1)S(1)}, u32[]{:S(2)}, u32[]{:S(2)}) %collective-permute-start.10) | collective-permute-done | bytes 294944 | tf_op jit(solution)/shard_map/ppermute | solution.py:281
  201.2 5.1 %collective-permute-done.11 = bf16[96,768]{1,0:T(8,128)(2,1)S(1)} collective-permute-done((bf16[96,768]{1,0:T(8,128)(2,1)S(1)}, bf16[96,768]{1,0:T(8,128)(2,1)S(1)}, u32[]{:S(2)}, u32[]{:S(2)}) %collective-permute-start.11) | collective-permute-done | bytes 147488 | tf_op jit(solution)/shard_map/ppermute | solution.py:281
  207.0 2.7 collective-permute-done.12
  210.5 2.6 collective-permute-start.15
  215.3 4.9 %collective-permute-done.16 = bf16[96,768]{1,0:T(8,128)(2,1)S(1)} collective-permute-done((bf16[96,768]{1,0:T(8,128)(2,1)S(1)}, bf16[96,768]{1,0:T(8,128)(2,1)S(1)}, u32[]{:S(2)}, u32[]{:S(2)}) %collective-permute-start.16) | collective-permute-done | bytes 147488 | tf_op jit(solution)/shard_map/ppermute | solution.py:281
  220.4 5.7 %collective-permute-done.17 = bf16[192,768]{1,0:T(8,128)(2,1)S(1)} collective-permute-done((bf16[192,768]{1,0:T(8,128)(2,1)S(1)}, bf16[192,768]{1,0:T(8,128)(2,1)S(1)}, u32[]{:S(2)}, u32[]{:S(2)}) %collective-permute-start.17) | collective-permute-done | bytes 294944 | tf_op jit(solution)/shard_map/ppermute | solution.py:281
  226.3 2.5 collective-permute-start.18
  236.7 3.8 %collective-permute-done.25 = bf16[192,768]{1,0:T(8,128)(2,1)S(1)} collective-permute-done((bf16[192,768]{1,0:T(8,128)(2,1)S(1)}, bf16[192,768]{1,0:T(8,128)(2,1)S(1)}, u32[]{:S(2)}, u32[]{:S(2)}) %collective-permute-start.25) | collective-permute-done | bytes 294944 | tf_op jit(solution)/shard_map/ppermute | solution.py:281
  242.8 15.7 %collective-permute-start.27 = (bf16[768,768]{1,0:T(8,128)(2,1)S(1)}, bf16[768,768]{1,0:T(8,128)(2,1)S(1)}, u32[]{:S(2)}, u32[]{:S(2)}) collective-permute-start(bf16[768,768]{1,0:T(8,128)(2,1)S(1)} %pad_maximum_fusion.7.k_mine.o_mine), channel_id=1, source_target_pairs={{0,16},{16,0},{32,48},{48,32},{64,80},{80,64},{96,112},{112,96},{1... | collective-permute-start | bytes 3538952 | tf_op jit(solution)/shard_map/ppermute | solution.py:320
  263.7 8.0 %finish.1 = (f32[768,768]{1,0:T(8,128)}, f32[768,768]{1,0:T(8,128)}, f32[768,768]{1,0:T(8,128)}, f32[768,768]{1,0:T(8,128)}) custom-call(s32[1]{0:T(128)} %bitcast.35.core_ref, bf16[768,768]{1,0:T(8,128)(2,1)} %copy-done.4, bf16[768,768]{1,0:T(8,128)(2,1)} %copy-done.3, bf16[768,768]{1,0:T(8,128)(2,1)} %copy-done.4, bf16[768,768]{1,0:T(8,128)(2,1)} %copy-done.3, ...), custom_call_target="tpu_custom_call" | custom-call | tf_op jit(solution)/shard_map/finish/pallas_call | solution.py:354
  (179 shorter events, 65.5 us)
Async XLA Ops:
  8.0 28.3 %all-to-all-start = ((bf16[16,96,512]{2,1,0:T(8,128)(2,1)}), bf16[16,96,512]{2,1,0:T(8,128)(2,1)S(1)}, u32[]{:S(2)}, u32[]{:S(2)}) async-start(bf16[16,96,512]{2,1,0:T(8,128)(2,1)} %bitcast.126), calls=%async_computation | async-start | bytes 3145728 | tf_op jit(solution)/shard_map/all_to_all | solution.py:387
  36.3 45.4 %all-to-all-start.2 = ((bf16[16,96,512]{2,1,0:T(8,128)(2,1)}), bf16[16,96,512]{2,1,0:T(8,128)(2,1)}, u32[]{:S(2)}, u32[]{:S(2)}) async-start(bf16[16,96,512]{2,1,0:T(8,128)(2,1)} %bitcast.128), calls=%async_computation.2 | async-start | bytes 3145728 | tf_op jit(solution)/shard_map/all_to_all | solution.py:387
  81.7 49.0 %all-to-all-start.1 = ((bf16[16,96,512]{2,1,0:T(8,128)(2,1)}), bf16[16,96,512]{2,1,0:T(8,128)(2,1)S(1)}, u32[]{:S(2)}, u32[]{:S(2)}) async-start(bf16[16,96,512]{2,1,0:T(8,128)(2,1)} %copy-done.1), calls=%async_computation.1 | async-start | bytes 3145728 | tf_op jit(solution)/shard_map/all_to_all | solution.py:387
  131.8 27.1 %all-to-all-start.3 = ((bf16[16,96,512]{2,1,0:T(8,128)(2,1)}), bf16[16,96,512]{2,1,0:T(8,128)(2,1)S(1)}, u32[]{:S(2)}, u32[]{:S(2)}) async-start(bf16[16,96,512]{2,1,0:T(8,128)(2,1)} %attend.3), calls=%async_computation.3 | async-start | bytes 3145728 | tf_op jit(solution)/shard_map/all_to_all | solution.py:387
  143.3 5.3 %collective-permute-start = (bf16[768,768]{1,0:T(8,128)(2,1)S(1)}, bf16[768,768]{1,0:T(8,128)(2,1)}, u32[]{:S(2)}, u32[]{:S(2)}) collective-permute-start(bf16[768,768]{1,0:T(8,128)(2,1)S(1)} %broadcast_select_fusion.1), channel_id=1, source_target_pairs={{0,16},{16,0},{32,48},{48,32},{64,80},{80,64},{96,112},{112,96},{1... | collective-permute-start | bytes 3538952 | tf_op jit(solution)/shard_map/ppermute | solution.py:290
  164.8 13.0 %collective-permute-start.3 = (bf16[192,768]{1,0:T(8,128)(2,1)S(1)}, bf16[192,768]{1,0:T(8,128)(2,1)S(1)}, u32[]{:S(2)}, u32[]{:S(2)}) collective-permute-start(bf16[192,768]{1,0:T(8,128)(2,1)S(1)} %get-tuple-element.40), channel_id=1, source_target_pairs={{0,32},{16,48},{32,0},{48,16},{64,96},{80,112},{96,64},{112,80},{1... | collective-permute-start | bytes 884744 | tf_op jit(solution)/shard_map/ppermute | solution.py:281
  167.9 9.9 %collective-permute-start.5 = (bf16[192,768]{1,0:T(8,128)(2,1)S(1)}, bf16[192,768]{1,0:T(8,128)(2,1)S(1)}, u32[]{:S(2)}, u32[]{:S(2)}) collective-permute-start(bf16[192,768]{1,0:T(8,128)(2,1)S(1)} %get-tuple-element.41), channel_id=1, source_target_pairs={{0,96},{16,112},{32,64},{48,80},{64,32},{80,48},{96,0},{112,16},{1... | collective-permute-start | bytes 884744 | tf_op jit(solution)/shard_map/ppermute | solution.py:281
  168.2 11.4 %collective-permute-start.1 = (bf16[768,768]{1,0:T(8,128)(2,1)S(1)}, bf16[768,768]{1,0:T(8,128)(2,1)S(1)}, u32[]{:S(2)}, u32[]{:S(2)}) collective-permute-start(bf16[768,768]{1,0:T(8,128)(2,1)S(1)} %broadcast_select_fusion), channel_id=1, source_target_pairs={{0,16},{16,0},{32,48},{48,32},{64,80},{80,64},{96,112},{112,96},{1... | collective-permute-start | bytes 3538952 | tf_op jit(solution)/shard_map/ppermute | solution.py:290
  178.3 5.3 %collective-permute-start.4 = (bf16[96,768]{1,0:T(8,128)(2,1)S(1)}, bf16[96,768]{1,0:T(8,128)(2,1)S(1)}, u32[]{:S(2)}, u32[]{:S(2)}) collective-permute-start(bf16[96,768]{1,0:T(8,128)(2,1)S(1)} %broadcast_select_fusion.29), channel_id=1, source_target_pairs={{0,96},{16,112},{32,64},{48,80},{64,32},{80,48},{96,0},{112,16},{1... | collective-permute-start | bytes 442376 | tf_op jit(solution)/shard_map/ppermute | solution.py:281
  180.2 6.2 %collective-permute-start.7 = (bf16[192,768]{1,0:T(8,128)(2,1)S(1)}, bf16[192,768]{1,0:T(8,128)(2,1)S(1)}, u32[]{:S(2)}, u32[]{:S(2)}) collective-permute-start(bf16[192,768]{1,0:T(8,128)(2,1)S(1)} %get-tuple-element.42), channel_id=1, source_target_pairs={{0,4},{1,5},{2,6},{3,7},{4,0},{5,1},{6,2},{7,3},{8,12},{9,13},{10,... | collective-permute-start | bytes 884744 | tf_op jit(solution)/shard_map/ppermute | solution.py:281
  183.6 6.9 %collective-permute-start.2 = (bf16[192,768]{1,0:T(8,128)(2,1)S(1)}, bf16[192,768]{1,0:T(8,128)(2,1)S(1)}, u32[]{:S(2)}, u32[]{:S(2)}) collective-permute-start(bf16[192,768]{1,0:T(8,128)(2,1)S(1)} %get-tuple-element.44), channel_id=1, source_target_pairs={{0,12},{1,13},{2,14},{3,15},{4,8},{5,9},{6,10},{7,11},{8,4},{9,5},... | collective-permute-start | bytes 884744 | tf_op jit(solution)/shard_map/ppermute | solution.py:281
  186.5 6.8 %collective-permute-start.8 = (bf16[96,768]{1,0:T(8,128)(2,1)S(1)}, bf16[96,768]{1,0:T(8,128)(2,1)S(1)}, u32[]{:S(2)}, u32[]{:S(2)}) collective-permute-start(bf16[96,768]{1,0:T(8,128)(2,1)S(1)} %broadcast_select_fusion.23), channel_id=1, source_target_pairs={{0,12},{1,13},{2,14},{3,15},{4,8},{5,9},{6,10},{7,11},{8,4},{9,5},... | collective-permute-start | bytes 442376 | tf_op jit(solution)/shard_map/ppermute | solution.py:281
  195.2 5.7 %collective-permute-start.10 = (bf16[192,768]{1,0:T(8,128)(2,1)S(1)}, bf16[192,768]{1,0:T(8,128)(2,1)S(1)}, u32[]{:S(2)}, u32[]{:S(2)}) collective-permute-start(bf16[192,768]{1,0:T(8,128)(2,1)S(1)} %bitcast.163), channel_id=1, source_target_pairs={{0,1},{1,0},{2,3},{3,2},{4,5},{5,4},{6,7},{7,6},{8,9},{9,8},{10,11... | collective-permute-start | bytes 884744 | tf_op jit(solution)/shard_map/ppermute | solution.py:281
  201.0 5.3 %collective-permute-start.11 = (bf16[96,768]{1,0:T(8,128)(2,1)S(1)}, bf16[96,768]{1,0:T(8,128)(2,1)S(1)}, u32[]{:S(2)}, u32[]{:S(2)}) collective-permute-start(bf16[96,768]{1,0:T(8,128)(2,1)S(1)} %broadcast_select_fusion.19), channel_id=1, source_target_pairs={{0,3},{1,2},{2,1},{3,0},{4,7},{5,6},{6,5},{7,4},{8,11},{9,10},{10,... | collective-permute-start | bytes 442376 | tf_op jit(solution)/shard_map/ppermute | solution.py:281
  214.9 5.3 %collective-permute-start.16 = (bf16[96,768]{1,0:T(8,128)(2,1)S(1)}, bf16[96,768]{1,0:T(8,128)(2,1)S(1)}, u32[]{:S(2)}, u32[]{:S(2)}) collective-permute-start(bf16[96,768]{1,0:T(8,128)(2,1)S(1)} %pad_maximum_fusion.15), channel_id=1, source_target_pairs={{0,3},{1,2},{2,1},{3,0},{4,7},{5,6},{6,5},{7,4},{8,11},{9,10},{10,... | collective-permute-start | bytes 442376 | tf_op jit(solution)/shard_map/ppermute | solution.py:281
  220.3 5.8 %collective-permute-start.17 = (bf16[192,768]{1,0:T(8,128)(2,1)S(1)}, bf16[192,768]{1,0:T(8,128)(2,1)S(1)}, u32[]{:S(2)}, u32[]{:S(2)}) collective-permute-start(bf16[192,768]{1,0:T(8,128)(2,1)S(1)} %pad_maximum_fusion.10), channel_id=1, source_target_pairs={{0,1},{1,0},{2,3},{3,2},{4,5},{5,4},{6,7},{7,6},{8,9},{9,8},{10,11... | collective-permute-start | bytes 884744 | tf_op jit(solution)/shard_map/ppermute | solution.py:281
  226.3 5.6 %collective-permute-start.18 = (bf16[96,768]{1,0:T(8,128)(2,1)S(1)}, bf16[96,768]{1,0:T(8,128)(2,1)S(1)}, u32[]{:S(2)}, u32[]{:S(2)}) collective-permute-start(bf16[96,768]{1,0:T(8,128)(2,1)S(1)} %bitcast.152), channel_id=1, source_target_pairs={{0,96},{16,112},{32,64},{48,80},{64,32},{80,48},{96,0},{112,16},{1... | collective-permute-start | bytes 442376 | tf_op jit(solution)/shard_map/ppermute | solution.py:281
  228.8 7.2 %collective-permute-start.20 = (bf16[96,768]{1,0:T(8,128)(2,1)S(1)}, bf16[96,768]{1,0:T(8,128)(2,1)S(1)}, u32[]{:S(2)}, u32[]{:S(2)}) collective-permute-start(bf16[96,768]{1,0:T(8,128)(2,1)S(1)} %bitcast.147), channel_id=1, source_target_pairs={{0,12},{1,13},{2,14},{3,15},{4,8},{5,9},{6,10},{7,11},{8,4},{9,5},... | collective-permute-start | bytes 442376 | tf_op jit(solution)/shard_map/ppermute | solution.py:281
  229.7 5.9 %collective-permute-start.22 = (bf16[96,768]{1,0:T(8,128)(2,1)S(1)}, bf16[96,768]{1,0:T(8,128)(2,1)S(1)}, u32[]{:S(2)}, u32[]{:S(2)}) collective-permute-start(bf16[96,768]{1,0:T(8,128)(2,1)S(1)} %bitcast.149), channel_id=1, source_target_pairs={{0,32},{16,48},{32,0},{48,16},{64,96},{80,112},{96,64},{112,80},{1... | collective-permute-start | bytes 442376 | tf_op jit(solution)/shard_map/ppermute | solution.py:281
  232.0 26.5 %collective-permute-start.19 = (bf16[192,768]{1,0:T(8,128)(2,1)S(1)}, bf16[192,768]{1,0:T(8,128)(2,1)S(1)}, u32[]{:S(2)}, u32[]{:S(2)}) collective-permute-start(bf16[192,768]{1,0:T(8,128)(2,1)S(1)} %pad_maximum_fusion.11), channel_id=1, source_target_pairs={{0,32},{16,48},{32,0},{48,16},{64,96},{80,112},{96,64},{112,80},{1... | collective-permute-start | bytes 884744 | tf_op jit(solution)/shard_map/ppermute | solution.py:281
  233.6 6.9 %collective-permute-start.25 = (bf16[192,768]{1,0:T(8,128)(2,1)S(1)}, bf16[192,768]{1,0:T(8,128)(2,1)S(1)}, u32[]{:S(2)}, u32[]{:S(2)}) collective-permute-start(bf16[192,768]{1,0:T(8,128)(2,1)S(1)} %pad_maximum_fusion.14), channel_id=1, source_target_pairs={{0,12},{1,13},{2,14},{3,15},{4,8},{5,9},{6,10},{7,11},{8,4},{9,5},... | collective-permute-start | bytes 884744 | tf_op jit(solution)/shard_map/ppermute | solution.py:281
  235.7 6.9 %collective-permute-start.23 = (bf16[192,768]{1,0:T(8,128)(2,1)S(1)}, bf16[192,768]{1,0:T(8,128)(2,1)S(1)}, u32[]{:S(2)}, u32[]{:S(2)}) collective-permute-start(bf16[192,768]{1,0:T(8,128)(2,1)S(1)} %pad_maximum_fusion.13), channel_id=1, source_target_pairs={{0,96},{16,112},{32,64},{48,80},{64,32},{80,48},{96,0},{112,16},{1... | collective-permute-start | bytes 884744 | tf_op jit(solution)/shard_map/ppermute | solution.py:281
  236.1 22.5 %collective-permute-start.21 = (bf16[192,768]{1,0:T(8,128)(2,1)S(1)}, bf16[192,768]{1,0:T(8,128)(2,1)S(1)}, u32[]{:S(2)}, u32[]{:S(2)}) collective-permute-start(bf16[192,768]{1,0:T(8,128)(2,1)S(1)} %pad_maximum_fusion.12), channel_id=1, source_target_pairs={{0,4},{1,5},{2,6},{3,7},{4,0},{5,1},{6,2},{7,3},{8,12},{9,13},{10,... | collective-permute-start | bytes 884744 | tf_op jit(solution)/shard_map/ppermute | solution.py:281
  242.8 18.2 %collective-permute-start.27 = (bf16[768,768]{1,0:T(8,128)(2,1)S(1)}, bf16[768,768]{1,0:T(8,128)(2,1)S(1)}, u32[]{:S(2)}, u32[]{:S(2)}) collective-permute-start(bf16[768,768]{1,0:T(8,128)(2,1)S(1)} %pad_maximum_fusion.7.k_mine.o_mine), channel_id=1, source_target_pairs={{0,16},{16,0},{32,48},{48,32},{64,80},{80,64},{96,112},{112,96},{1... | collective-permute-start | bytes 3538952 | tf_op jit(solution)/shard_map/ppermute | solution.py:320
  (38 other events, 128.4 us)
